TPU v7x, 32 devices: a whole 2x2x4 slice. The times are simulated.
32 devices in a mesh: section: 2 (over y), row: 16 (over z, x, core).
Axes of the slice: x: 2, y: 2, z: 4, core: 2. Of those that a mesh axis runs over, the one named last changes fastest.
Arguments:
- pair: bfloat16 [2, 128, 128, 128], P(None, 'row'), may hold values from -6 to 6
- valid_tokens: int32 [2], replicated, may hold values from 32 to 128, as said below
- crop_order: int32 [2], replicated, may hold values from 0 to 1, each once
- w_proj: bfloat16 [2, 128, 384], P('section'), may hold values from -0.5 to 0.5
- w_out: bfloat16 [2, 64, 128], P('section'), may hold values from -0.75 to 0.75
- w_in: bfloat16 [2, 128, 1024], P('section'), may hold values from -0.5 to 0.5
- w_back: bfloat16 [2, 512, 128], P('section'), may hold values from -0.25 to 0.25
Outputs:
- final_pair: bfloat16 [2, 128, 128, 128], P('section', 'row')
Inputs may be any that keep to these rules, and one draw needn't show every extreme that they name: `valid_tokens`: valid tokens of each crop; some crop is full and some other has 32. `crop_order`: each crop is taken at exactly one slot.
All inputs are finite; a program needn't handle non-finite values.
Results may differ from a plain program's by a relative error of at most 0.015.
Values may be sent and summed in bfloat16 or wider, within the bound.
No kernel may reach another device: no remote copies, remote signals or barrier semaphores. Data moves between devices by JAX's collectives and lax.ppermute only.
A program may use at most 64 MiB of HBM per device.

v0:
```python
import jax
import jax.numpy as jnp
from jax import lax
from jax.sharding import PartitionSpec as P


def layer_norm(value):
    mean = jnp.mean(value, -1, keepdims=True)
    centred = value - mean
    var = jnp.mean(centred * centred, -1, keepdims=True)
    return centred * lax.rsqrt(var + 1e-05)


def pair_block(state, valid, row_start, w_proj, w_out, w_in, w_back):
    rows_here = state.shape[0]
    count = state.shape[1]
    width = state.shape[2]
    inner = w_out.shape[0]
    trans = w_back.shape[0]
    normed = (
        layer_norm(state.astype(jnp.float32)).astype(jnp.bfloat16).reshape(rows_here * count, width)
    )
    proj = jnp.dot(normed, w_proj, preferred_element_type=jnp.float32).reshape(rows_here, count, -1)
    keep_cols = (jnp.arange(count) < valid).astype(jnp.float32)
    keep_rows = (row_start + jnp.arange(rows_here) < valid).astype(jnp.float32)
    mask = keep_rows[:, None, None] * keep_cols[None, :, None]
    left = (mask * jax.nn.sigmoid(proj[..., inner : 2 * inner]) * proj[..., :inner]).astype(
        jnp.bfloat16
    )
    right = (
        mask * jax.nn.sigmoid(proj[..., 3 * inner : 4 * inner]) * proj[..., 2 * inner : 3 * inner]
    ).astype(jnp.bfloat16)
    gate = jax.nn.sigmoid(proj[..., 4 * inner :])
    left_whole, right_whole = (
        lax.all_to_all(left, "row", split_axis=2, concat_axis=0, tiled=True),
        lax.all_to_all(right, "row", split_axis=2, concat_axis=0, tiled=True),
    )
    tri_part = jnp.einsum(
        "ikc,jkc->ijc", left_whole, right_whole, preferred_element_type=jnp.float32
    )
    tri = lax.all_to_all(
        tri_part.astype(jnp.bfloat16), "row", split_axis=0, concat_axis=2, tiled=True
    ).astype(tri_part.dtype)
    tri_normed = layer_norm(tri).astype(jnp.bfloat16).reshape(rows_here * count, inner)
    update = jnp.dot(tri_normed, w_out, preferred_element_type=jnp.float32).reshape(
        rows_here, count, width
    )
    first = (state.astype(jnp.float32) + gate * update).astype(jnp.bfloat16)
    second = (
        layer_norm(first.astype(jnp.float32)).astype(jnp.bfloat16).reshape(rows_here * count, width)
    )
    hidden = jnp.dot(second, w_in, preferred_element_type=jnp.float32)
    act = (jax.nn.silu(hidden[:, :trans]) * hidden[:, trans:]).astype(jnp.bfloat16)
    back = jnp.dot(act, w_back, preferred_element_type=jnp.float32).reshape(rows_here, count, width)
    return (first.astype(jnp.float32) + back).astype(jnp.bfloat16)


def on_device(pair, valid_tokens, crop_order, w_proj, w_out, w_in, w_back):
    crops = pair.shape[0]
    rows_here = pair.shape[1]
    row_start = lax.axis_index("row") * rows_here
    sections = lax.axis_size("section")
    section = lax.axis_index("section")
    share = crops // sections
    all_proj, all_out, all_in, all_back = (
        lax.all_gather(w_proj, "section", axis=0, tiled=True),
        lax.all_gather(w_out, "section", axis=0, tiled=True),
        lax.all_gather(w_in, "section", axis=0, tiled=True),
        lax.all_gather(w_back, "section", axis=0, tiled=True),
    )
    blocks = all_proj.shape[0]

    def one_crop(index, outputs):
        crop = crop_order[section * share + index]
        valid = valid_tokens[crop]
        state = lax.dynamic_index_in_dim(pair, crop, 0, keepdims=False)

        def apply_block(block, value):
            return pair_block(
                value,
                valid,
                row_start,
                all_proj[block],
                all_out[block],
                all_in[block],
                all_back[block],
            )

        final = lax.fori_loop(0, blocks, apply_block, state)
        return lax.dynamic_update_index_in_dim(outputs, final, index, 0)

    empty = jnp.zeros((share,) + pair.shape[1:], jnp.bfloat16)
    return lax.fori_loop(0, share, one_crop, empty)


def solution(mesh):
    in_specs = (
        P(None, "row", None, None),
        P(),
        P(),
        P("section", None, None),
        P("section", None, None),
        P("section", None, None),
        P("section", None, None),
    )
    out_specs = P("section", "row", None, None)
    return jax.shard_map(
        on_device, mesh=mesh, in_specs=in_specs, out_specs=out_specs, check_vma=False
    )
```

profile of v0, /device:TPU:0, one launch (start us, length us, event | category | flops | bytes accessed | tf_op | source)
XLA Modules:
  0.0 133.9 jit_solution(968022301504030877)
XLA Ops:
  0.0 1.3 dynamic_slice.41
  3.3 1.2 dynamic_slice.43
  4.5 13.2 %all_gather.14 = bf16[2,128,1024]{2,1,0:T(8,128)(2,1)} all-gather(bf16[1,128,1024]{2,1,0:T(8,128)(2,1)} %param.14), channel_id=1, replica_groups=mesh['section'=2,'row'=16] {'section'}, dimensions={0}, use_global_device_ids=true | all-gather | bytes 786432 | tf_op jit(solution)/shard_map/all_gather | solution.py:68
  17.7 5.9 %all_gather.15 = bf16[2,512,128]{2,1,0:T(8,128)(2,1)} all-gather(bf16[1,512,128]{2,1,0:T(8,128)(2,1)} %param.15), channel_id=1, replica_groups=mesh['section'=2,'row'=16] {'section'}, dimensions={0}, use_global_device_ids=true | all-gather | bytes 393216 | tf_op jit(solution)/shard_map/all_gather | solution.py:69
  23.6 5.5 %all_gather.12 = bf16[2,128,384]{2,1,0:T(8,128)(2,1)S(1)} all-gather(bf16[1,128,384]{2,1,0:T(8,128)(2,1)} %param.12), channel_id=1, replica_groups=mesh['section'=2,'row'=16] {'section'}, dimensions={0}, use_global_device_ids=true | all-gather | bytes 294912 | tf_op jit(solution)/shard_map/all_gather | solution.py:66
  29.1 4.6 %all_gather.13 = bf16[2,64,128]{2,1,0:T(8,128)(2,1)S(1)} all-gather(bf16[1,64,128]{2,1,0:T(8,128)(2,1)} %param.13), channel_id=1, replica_groups=mesh['section'=2,'row'=16] {'section'}, dimensions={0}, use_global_device_ids=true | all-gather | bytes 49152 | tf_op jit(solution)/shard_map/all_gather | solution.py:67
  33.7 99.5 %while.21 = (s32[]{:T(128)}, bf16[8,128,128]{2,1,0:T(8,128)(2,1)S(1)}, bf16[2,128,384]{2,1,0:T(8,128)(2,1)S(1)}, s32[]{:T(128)}, s32[]{:T(128)}, /*index=5*/bf16...) while((s32[]{:T(128)}, ...), condition=%wide.region_7.8_spmd, body=%wide.region_0.7_spmd.sunk | while | flops 545067264 | bytes 30512496 | solution.py:89
  34.4 0.5 fusion.73
  34.9 1.4 %fusion.74 = (f32[8,128,64]{2,1,0:T(8,128)}, f32[8,128,64]{2,1,0:T(8,128)S(1)}, f32[8,128,64]{2,1,0:T(8,128)}, f32[8,128,64]{2,1,0:T(8,128)S(1)}) fusion(f32[8,128,384]{2,1,0:T(8,128)S(1)} %fusion.73), kind=kLoop, calls=%fused_computation.62.clone.1 | loop fusion | bytes 2097152 | tf_op jit(solution)/shard_map/while/body/eval_jaxpr/while/body/eval_jaxpr/slice | solution.py:31
  36.2 1.9 %copy.84 = f32[8,128,64]{1,2,0:T(8,128)} copy(f32[8,128,64]{2,1,0:T(8,128)} %get-tuple-element.272) | data formatting | bytes 524288 | tf_op jit(solution)/shard_map/while/body/eval_jaxpr/while
  38.2 1.9 %copy.85 = f32[8,128,64]{1,2,0:T(8,128)} copy(f32[8,128,64]{2,1,0:T(8,128)} %get-tuple-element.273) | data formatting | bytes 524288 | tf_op jit(solution)/shard_map/while/body/eval_jaxpr/while
  40.1 0.9 copy.86
  41.2 0.5 compare_convert_fusion.4
  41.8 0.5 compare_convert_fusion.5
  42.4 1.3 multiply_convert_fusion.5
  43.6 0.7 copy.88
  44.4 5.9 %all-to-all-start = ((bf16[8,128,64]{1,0,2:T(8,128)(2,1)}), bf16[8,128,64]{1,0,2:T(8,128)(2,1)S(1)}, u32[]{:S(2)}, u32[]{:S(2)}) async-start(bf16[8,128,64]{1,0,2:T(8,128)(2,1)} %copy.88), calls=%async_computation | async-start | bytes 262144 | tf_op jit(solution)/shard_map/while/body/eval_jaxpr/while/body/eval_jaxpr/all_to_all | solution.py:35
  50.4 7.8 %all-to-all-done = bf16[8,128,64]{1,0,2:T(8,128)(2,1)S(1)} async-done(((bf16[8,128,64]{1,0,2:T(8,128)(2,1)}), bf16[8,128,64]{1,0,2:T(8,128)(2,1)S(1)}, u32[]{:S(2)}, u32[]{:S(2)}) %all-to-all-start) | async-done | bytes 131104 | tf_op jit(solution)/shard_map/while/body/eval_jaxpr/while/body/eval_jaxpr/all_to_all | solution.py:35
  58.2 10.5 %all_to_all.88 = bf16[8,128,64]{1,0,2:T(8,128)(2,1)S(1)} all-to-all(bf16[8,128,64]{1,0,2:T(8,128)(2,1)S(1)} %copy.89), channel_id=1, replica_groups=mesh['section'=2,'row'=16] {'row'}, dimensions={2} | all-to-all | bytes 262144 | tf_op jit(solution)/shard_map/while/body/eval_jaxpr/while/body/eval_jaxpr/all_to_all | solution.py:36
  68.9 0.8 copy.90
  69.7 3.5 %all-to-all-start.2 = ((bf16[128,128,4]{1,2,0:T(4,128)(2,1)}), bf16[128,128,4]{1,2,0:T(4,128)(2,1)S(1)}, u32[]{:S(2)}, u32[]{:S(2)}) async-start(bf16[128,128,4]{1,2,0:T(4,128)(2,1)} %copy.90), calls=%async_computation.2 | async-start | bytes 262144 | tf_op jit(solution)/shard_map/while/body/eval_jaxpr/while/body/eval_jaxpr/all_to_all | solution.py:41
  73.2 7.9 %all-to-all-done.2 = bf16[128,128,4]{1,2,0:T(4,128)(2,1)S(1)} async-done(((bf16[128,128,4]{1,2,0:T(4,128)(2,1)}), bf16[128,128,4]{1,2,0:T(4,128)(2,1)S(1)}, u32[]{:S(2)}, u32[]{:S(2)}) %all-to-all-start.2) | async-done | bytes 131104 | tf_op jit(solution)/shard_map/while/body/eval_jaxpr/while/body/eval_jaxpr/all_to_all | solution.py:41
  81.3 0.4 fusion.79
  81.8 0.4 multiply_reduce_fusion.2
  82.5 0.7 fusion.80
  83.3 0.7 fusion.81
  84.2 0.4 fusion.82
  85.3 0.5 fusion.73
  85.8 1.4 %fusion.74 = (f32[8,128,64]{2,1,0:T(8,128)}, f32[8,128,64]{2,1,0:T(8,128)S(1)}, f32[8,128,64]{2,1,0:T(8,128)}, f32[8,128,64]{2,1,0:T(8,128)S(1)}) fusion(f32[8,128,384]{2,1,0:T(8,128)S(1)} %fusion.73), kind=kLoop, calls=%fused_computation.62.clone.1 | loop fusion | bytes 2097152 | tf_op jit(solution)/shard_map/while/body/eval_jaxpr/while/body/eval_jaxpr/slice | solution.py:31
  87.2 1.9 %copy.84 = f32[8,128,64]{1,2,0:T(8,128)} copy(f32[8,128,64]{2,1,0:T(8,128)} %get-tuple-element.272) | data formatting | bytes 524288 | tf_op jit(solution)/shard_map/while/body/eval_jaxpr/while
  89.1 1.9 %copy.85 = f32[8,128,64]{1,2,0:T(8,128)} copy(f32[8,128,64]{2,1,0:T(8,128)} %get-tuple-element.273) | data formatting | bytes 524288 | tf_op jit(solution)/shard_map/while/body/eval_jaxpr/while
  91.1 0.9 copy.86
  92.2 0.5 compare_convert_fusion.4
  92.7 0.5 compare_convert_fusion.5
  93.3 1.3 multiply_convert_fusion.5
  94.6 0.7 copy.88
  95.3 3.5 %all-to-all-start = ((bf16[8,128,64]{1,0,2:T(8,128)(2,1)}), bf16[8,128,64]{1,0,2:T(8,128)(2,1)S(1)}, u32[]{:S(2)}, u32[]{:S(2)}) async-start(bf16[8,128,64]{1,0,2:T(8,128)(2,1)} %copy.88), calls=%async_computation | async-start | bytes 262144 | tf_op jit(solution)/shard_map/while/body/eval_jaxpr/while/body/eval_jaxpr/all_to_all | solution.py:35
  99.0 7.8 %all-to-all-done = bf16[8,128,64]{1,0,2:T(8,128)(2,1)S(1)} async-done(((bf16[8,128,64]{1,0,2:T(8,128)(2,1)}), bf16[8,128,64]{1,0,2:T(8,128)(2,1)S(1)}, u32[]{:S(2)}, u32[]{:S(2)}) %all-to-all-start) | async-done | bytes 131104 | tf_op jit(solution)/shard_map/while/body/eval_jaxpr/while/body/eval_jaxpr/all_to_all | solution.py:35
  106.7 10.5 %all_to_all.88 = bf16[8,128,64]{1,0,2:T(8,128)(2,1)S(1)} all-to-all(bf16[8,128,64]{1,0,2:T(8,128)(2,1)S(1)} %copy.89), channel_id=1, replica_groups=mesh['section'=2,'row'=16] {'row'}, dimensions={2} | all-to-all | bytes 262144 | tf_op jit(solution)/shard_map/while/body/eval_jaxpr/while/body/eval_jaxpr/all_to_all | solution.py:36
  117.4 0.8 copy.90
  118.2 3.5 %all-to-all-start.2 = ((bf16[128,128,4]{1,2,0:T(4,128)(2,1)}), bf16[128,128,4]{1,2,0:T(4,128)(2,1)S(1)}, u32[]{:S(2)}, u32[]{:S(2)}) async-start(bf16[128,128,4]{1,2,0:T(4,128)(2,1)} %copy.90), calls=%async_computation.2 | async-start | bytes 262144 | tf_op jit(solution)/shard_map/while/body/eval_jaxpr/while/body/eval_jaxpr/all_to_all | solution.py:41
  121.7 7.9 %all-to-all-done.2 = bf16[128,128,4]{1,2,0:T(4,128)(2,1)S(1)} async-done(((bf16[128,128,4]{1,2,0:T(4,128)(2,1)}), bf16[128,128,4]{1,2,0:T(4,128)(2,1)S(1)}, u32[]{:S(2)}, u32[]{:S(2)}) %all-to-all-start.2) | async-done | bytes 131104 | tf_op jit(solution)/shard_map/while/body/eval_jaxpr/while/body/eval_jaxpr/all_to_all | solution.py:41
  129.9 0.4 fusion.79
  130.3 0.4 multiply_reduce_fusion.2
  131.0 0.7 fusion.80
  131.8 0.7 fusion.81
  132.7 0.4 fusion.82
  133.2 0.7 copy-done.1
  (54 shorter events, 4.0 us)
Async XLA Ops:
  0.0 3.2 %copy-start = (bf16[2,8,128,128]{3,2,1,0:T(8,128)(2,1)S(1)}, bf16[2,8,128,128]{3,2,1,0:T(8,128)(2,1)}, u32[]{:S(2)}) copy-start(bf16[2,8,128,128]{3,2,1,0:T(8,128)(2,1)} %param.9) | copy-start | bytes 1572868
  33.7 0.7 copy-start.4
  44.4 13.8 %all-to-all-start = ((bf16[8,128,64]{1,0,2:T(8,128)(2,1)}), bf16[8,128,64]{1,0,2:T(8,128)(2,1)S(1)}, u32[]{:S(2)}, u32[]{:S(2)}) async-start(bf16[8,128,64]{1,0,2:T(8,128)(2,1)} %copy.88), calls=%async_computation | async-start | bytes 262144 | tf_op jit(solution)/shard_map/while/body/eval_jaxpr/while/body/eval_jaxpr/all_to_all | solution.py:35
  69.7 11.4 %all-to-all-start.2 = ((bf16[128,128,4]{1,2,0:T(4,128)(2,1)}), bf16[128,128,4]{1,2,0:T(4,128)(2,1)S(1)}, u32[]{:S(2)}, u32[]{:S(2)}) async-start(bf16[128,128,4]{1,2,0:T(4,128)(2,1)} %copy.90), calls=%async_computation.2 | async-start | bytes 262144 | tf_op jit(solution)/shard_map/while/body/eval_jaxpr/while/body/eval_jaxpr/all_to_all | solution.py:41
  81.3 1.2 copy-start.2
  83.2 1.0 copy-start.3
  83.2 1.4 %copy-start.5 = (bf16[2,128,384]{2,1,0:T(8,128)(2,1)S(1)}, bf16[2,128,384]{2,1,0:T(8,128)(2,1)}, u32[]{:S(2)}) copy-start(bf16[2,128,384]{2,1,0:T(8,128)(2,1)} %copy-done.4) | copy-start | bytes 589828 | tf_op jit(solution)/shard_map/while/body/eval_jaxpr/while
  84.7 0.7 copy-start.4
  95.3 11.4 %all-to-all-start = ((bf16[8,128,64]{1,0,2:T(8,128)(2,1)}), bf16[8,128,64]{1,0,2:T(8,128)(2,1)S(1)}, u32[]{:S(2)}, u32[]{:S(2)}) async-start(bf16[8,128,64]{1,0,2:T(8,128)(2,1)} %copy.88), calls=%async_computation | async-start | bytes 262144 | tf_op jit(solution)/shard_map/while/body/eval_jaxpr/while/body/eval_jaxpr/all_to_all | solution.py:35
  118.2 11.4 %all-to-all-start.2 = ((bf16[128,128,4]{1,2,0:T(4,128)(2,1)}), bf16[128,128,4]{1,2,0:T(4,128)(2,1)S(1)}, u32[]{:S(2)}, u32[]{:S(2)}) async-start(bf16[128,128,4]{1,2,0:T(4,128)(2,1)} %copy.90), calls=%async_computation.2 | async-start | bytes 262144 | tf_op jit(solution)/shard_map/while/body/eval_jaxpr/while/body/eval_jaxpr/all_to_all | solution.py:41
  129.8 1.2 copy-start.2
  131.8 1.0 copy-start.3
  131.8 1.4 %copy-start.5 = (bf16[2,128,384]{2,1,0:T(8,128)(2,1)S(1)}, bf16[2,128,384]{2,1,0:T(8,128)(2,1)}, u32[]{:S(2)}) copy-start(bf16[2,128,384]{2,1,0:T(8,128)(2,1)} %copy-done.4) | copy-start | bytes 589828 | tf_op jit(solution)/shard_map/while/body/eval_jaxpr/while
  133.2 0.7 copy-start.1
where the time goes:
time: 135 us; the launch traced here: 134 us
  blocking collectives  50.2 us (37%)
  waiting for transfers between devices  31.3 us (23%)
  local copies, waits for them, and re-layouts  19.9 us (15%)
  starting transfers between devices  16.4 us (12%)
  other arithmetic  9.13 us (7%)
  matrix products  4.56 us (3%)
  between operations  1.98 us (1%)
    all_to_all x2, blocking collectives, pair_block(): lax.all_to_all(right, 'row', split_axis=2, concat_axis=0, tiled=True)  21 us
    all_to_all x2, waiting for transfers between devices, pair_block(): lax.all_to_all(tri_part.astype(jnp.bfloat16), 'row', split_axis=0, concat...  15.7 us
    all_to_all x2, waiting for transfers between devices, pair_block(): lax.all_to_all(left, 'row', split_axis=2, concat_axis=0, tiled=True)  15.6 us
    all_gather x1, blocking collectives, on_device(): lax.all_gather(w_in, 'section', axis=0, tiled=True)  13.2 us
    while x24, local copies, waits for them, and re-layouts  10.6 us
    all_to_all x2, starting transfers between devices, pair_block(): lax.all_to_all(left, 'row', split_axis=2, concat_axis=0, tiled=True)  9.42 us
    all_to_all x2, starting transfers between devices, pair_block(): lax.all_to_all(tri_part.astype(jnp.bfloat16), 'row', split_axis=0, concat...  7.03 us
    all_gather x1, blocking collectives, on_device(): lax.all_gather(w_back, 'section', axis=0, tiled=True)  5.94 us
  transfers between devices with their start and end apart: 4, of which 4 were waited for; matrix products, arithmetic and copies ran while one was open for 0% of the time, Pallas kernels for 0%

commit v1 on v0

--- a/solution.py
+++ b/solution.py
@@ -2,6 +2,20 @@
 import jax.numpy as jnp
 from jax import lax
 from jax.sharding import PartitionSpec as P
+
+
+def step_on_modes(m, array_axis):
+    dev_axis = "section"
+    z = lax.axis_size(dev_axis)
+    carry_in = lax.axis_index(dev_axis)
+    z1, arr_next, v_next = (z, carry_in, m.shape[array_axis])
+    z2, u_next = (m, 1)
+    while u_next < z1:
+        all_values = tuple(((ix, (ix - u_next) % z1) for ix in range(z1)))
+        current_arr = lax.ppermute(z2, axis_name=dev_axis, perm=all_values)
+        z2 = jnp.concatenate([z2, current_arr], array_axis)
+        u_next = 2 * u_next
+    return jnp.roll(z2, arr_next * v_next, axis=array_axis)
 
 
 def layer_norm(value):
@@ -65,7 +79,7 @@
     all_proj, all_out, all_in, all_back = (
         lax.all_gather(w_proj, "section", axis=0, tiled=True),
         lax.all_gather(w_out, "section", axis=0, tiled=True),
-        lax.all_gather(w_in, "section", axis=0, tiled=True),
+        step_on_modes(w_in, 0),
         lax.all_gather(w_back, "section", axis=0, tiled=True),
     )
     blocks = all_proj.shape[0]

time: 135 us -> 127 us (0.941)
  blocking collectives: 50.2 us -> 37 us
  starting transfers between devices: 16.4 us -> 19.4 us
  other arithmetic: 9.13 us -> 11.2 us
    all_gather x1 -> x0, blocking collectives: 13.2 us -> none  [on_device(): lax.all_gather(w_in, 'section', axis=0, tiled=True)]
    ppermute x0 -> x1, starting transfers between devices: none -> 3 us  [step_on_modes(): current_arr = lax.ppermute(z2, axis_name=dev_axis, perm=all_values)]
    concatenate x0 -> x1, other arithmetic: none -> 2.12 us  [step_on_modes(): return jnp.roll(z2, arr_next * v_next, axis=array_axis)]
  transfers between devices with their start and end apart: 4 -> 5, of which waited for: 4 -> 4; matrix products, arithmetic and copies ran while one was open for 0% -> 2% of each run, Pallas kernels for 0% -> 0%
where the time goes in v1:
time: 127 us; the launch traced here: 126 us
  blocking collectives  37 us (29%)
  waiting for transfers between devices  31.3 us (25%)
  local copies, waits for them, and re-layouts  19.8 us (16%)
  starting transfers between devices  19.4 us (15%)
  other arithmetic  11.2 us (9%)
  matrix products  4.57 us (4%)
  between operations  1.99 us (2%)
    all_to_all x2, blocking collectives, pair_block(): lax.all_to_all(right, 'row', split_axis=2, concat_axis=0, tiled=True)  21 us
    all_to_all x2, waiting for transfers between devices, pair_block(): lax.all_to_all(tri_part.astype(jnp.bfloat16), 'row', split_axis=0, concat...  15.7 us
    all_to_all x2, waiting for transfers between devices, pair_block(): lax.all_to_all(left, 'row', split_axis=2, concat_axis=0, tiled=True)  15.6 us
    while x24, local copies, waits for them, and re-layouts  10.6 us
    all_to_all x2, starting transfers between devices, pair_block(): lax.all_to_all(left, 'row', split_axis=2, concat_axis=0, tiled=True)  9.42 us
    all_to_all x2, starting transfers between devices, pair_block(): lax.all_to_all(tri_part.astype(jnp.bfloat16), 'row', split_axis=0, concat...  7.03 us
    all_gather x1, blocking collectives, on_device(): lax.all_gather(w_back, 'section', axis=0, tiled=True)  5.94 us
    all_gather x1, blocking collectives, on_device(): lax.all_gather(w_proj, 'section', axis=0, tiled=True)  5.48 us
  transfers between devices with their start and end apart: 5, of which 4 were waited for; matrix products, arithmetic and copies ran while one was open for 2% of the time, Pallas kernels for 0%

profile of v1, /device:TPU:0, one launch (start us, length us, event | category | flops | bytes accessed | tf_op | source)
XLA Modules:
  0.0 125.8 jit_solution(17041446096462136765)
XLA Ops:
  0.0 3.0 %collective-permute-start = (bf16[1,128,1024]{2,1,0:T(8,128)(2,1)}, bf16[1,128,1024]{2,1,0:T(8,128)(2,1)S(1)}, u32[]{:S(2)}, u32[]{:S(2)}) collective-permute-start(bf16[1,128,1024]{2,1,0:T(8,128)(2,1)} %param.14), channel_id=1, source_target_pairs={{0,16},{16,0},{1,17},{17,1},{2,18},{18,2},{3,19},{19,3},{4,20},{20... | collective-permute-start | bytes 786440 | tf_op jit(solution)/shard_map/ppermute | solution.py:15
  3.0 1.2 dynamic_slice.45
  6.2 1.2 dynamic_slice.47
  7.4 4.6 %all_gather.10 = bf16[2,64,128]{2,1,0:T(8,128)(2,1)S(1)} all-gather(bf16[1,64,128]{2,1,0:T(8,128)(2,1)} %param.13), channel_id=1, replica_groups=mesh['section'=2,'row'=16] {'section'}, dimensions={0}, use_global_device_ids=true | all-gather | bytes 49152 | tf_op jit(solution)/shard_map/all_gather | solution.py:81
  12.0 5.5 %all_gather.9 = bf16[2,128,384]{2,1,0:T(8,128)(2,1)S(1)} all-gather(bf16[1,128,384]{2,1,0:T(8,128)(2,1)} %param.12), channel_id=1, replica_groups=mesh['section'=2,'row'=16] {'section'}, dimensions={0}, use_global_device_ids=true | all-gather | bytes 294912 | tf_op jit(solution)/shard_map/all_gather | solution.py:80
  17.5 5.9 %all_gather.11 = bf16[2,512,128]{2,1,0:T(8,128)(2,1)} all-gather(bf16[1,512,128]{2,1,0:T(8,128)(2,1)} %param.15), channel_id=1, replica_groups=mesh['section'=2,'row'=16] {'section'}, dimensions={0}, use_global_device_ids=true | all-gather | bytes 393216 | tf_op jit(solution)/shard_map/all_gather | solution.py:83
  23.5 2.1 %fusion.43 = bf16[2,128,1024]{2,1,0:T(8,128)(2,1)} fusion(s32[]{:T(128)S(6)} %select_n.37, bf16[1,128,1024]{2,1,0:T(8,128)(2,1)} %param.14, bf16[1,128,1024]{2,1,0:T(8,128)(2,1)S(1)} %collective-permute-done), kind=kLoop, calls=%fused_computation.67 | loop fusion | flops 786432 | bytes 1048580 | tf_op jit(solution)/shard_map/jit(_roll_dynamic)/concatenate | solution.py:18
  25.6 99.5 %while.21 = (s32[]{:T(128)}, bf16[8,128,128]{2,1,0:T(8,128)(2,1)S(1)}, bf16[2,128,384]{2,1,0:T(8,128)(2,1)S(1)}, s32[]{:T(128)}, s32[]{:T(128)}, /*index=5*/bf16...) while((s32[]{:T(128)}, ...), condition=%wide.region_7.8_spmd, body=%wide.region_0.7_spmd.sunk | while | flops 545067264 | bytes 30512496 | solution.py:103
  26.3 0.5 fusion.76
  26.8 1.4 %fusion.77 = (f32[8,128,64]{2,1,0:T(8,128)}, f32[8,128,64]{2,1,0:T(8,128)S(1)}, f32[8,128,64]{2,1,0:T(8,128)}, f32[8,128,64]{2,1,0:T(8,128)S(1)}) fusion(f32[8,128,384]{2,1,0:T(8,128)S(1)} %fusion.76), kind=kLoop, calls=%fused_computation.69.clone.1 | loop fusion | bytes 2097152 | tf_op jit(solution)/shard_map/while/body/eval_jaxpr/while/body/eval_jaxpr/slice | solution.py:45
  28.1 1.9 %copy.84 = f32[8,128,64]{1,2,0:T(8,128)} copy(f32[8,128,64]{2,1,0:T(8,128)} %get-tuple-element.272) | data formatting | bytes 524288 | tf_op jit(solution)/shard_map/while/body/eval_jaxpr/while
  30.1 1.9 %copy.85 = f32[8,128,64]{1,2,0:T(8,128)} copy(f32[8,128,64]{2,1,0:T(8,128)} %get-tuple-element.273) | data formatting | bytes 524288 | tf_op jit(solution)/shard_map/while/body/eval_jaxpr/while
  32.0 0.9 copy.86
  33.1 0.5 compare_convert_fusion.4
  33.6 0.5 compare_convert_fusion.5
  34.3 1.3 multiply_convert_fusion.5
  35.5 0.7 copy.88
  36.3 5.9 %all-to-all-start = ((bf16[8,128,64]{1,0,2:T(8,128)(2,1)}), bf16[8,128,64]{1,0,2:T(8,128)(2,1)S(1)}, u32[]{:S(2)}, u32[]{:S(2)}) async-start(bf16[8,128,64]{1,0,2:T(8,128)(2,1)} %copy.88), calls=%async_computation | async-start | bytes 262144 | tf_op jit(solution)/shard_map/while/body/eval_jaxpr/while/body/eval_jaxpr/all_to_all | solution.py:49
  42.3 7.8 %all-to-all-done = bf16[8,128,64]{1,0,2:T(8,128)(2,1)S(1)} async-done(((bf16[8,128,64]{1,0,2:T(8,128)(2,1)}), bf16[8,128,64]{1,0,2:T(8,128)(2,1)S(1)}, u32[]{:S(2)}, u32[]{:S(2)}) %all-to-all-start) | async-done | bytes 131104 | tf_op jit(solution)/shard_map/while/body/eval_jaxpr/while/body/eval_jaxpr/all_to_all | solution.py:49
  50.1 10.5 %all_to_all.88 = bf16[8,128,64]{1,0,2:T(8,128)(2,1)S(1)} all-to-all(bf16[8,128,64]{1,0,2:T(8,128)(2,1)S(1)} %copy.89), channel_id=1, replica_groups=mesh['section'=2,'row'=16] {'row'}, dimensions={2} | all-to-all | bytes 262144 | tf_op jit(solution)/shard_map/while/body/eval_jaxpr/while/body/eval_jaxpr/all_to_all | solution.py:50
  60.8 0.8 copy.90
  61.6 3.5 %all-to-all-start.2 = ((bf16[128,128,4]{1,2,0:T(4,128)(2,1)}), bf16[128,128,4]{1,2,0:T(4,128)(2,1)S(1)}, u32[]{:S(2)}, u32[]{:S(2)}) async-start(bf16[128,128,4]{1,2,0:T(4,128)(2,1)} %copy.90), calls=%async_computation.2 | async-start | bytes 262144 | tf_op jit(solution)/shard_map/while/body/eval_jaxpr/while/body/eval_jaxpr/all_to_all | solution.py:55
  65.1 7.9 %all-to-all-done.2 = bf16[128,128,4]{1,2,0:T(4,128)(2,1)S(1)} async-done(((bf16[128,128,4]{1,2,0:T(4,128)(2,1)}), bf16[128,128,4]{1,2,0:T(4,128)(2,1)S(1)}, u32[]{:S(2)}, u32[]{:S(2)}) %all-to-all-start.2) | async-done | bytes 131104 | tf_op jit(solution)/shard_map/while/body/eval_jaxpr/while/body/eval_jaxpr/all_to_all | solution.py:55
  73.2 0.4 fusion.82
  73.7 0.4 multiply_reduce_fusion.2
  74.4 0.7 fusion.83
  75.1 0.7 fusion.84
  76.1 0.4 fusion.85
  77.2 0.5 fusion.76
  77.7 1.4 %fusion.77 = (f32[8,128,64]{2,1,0:T(8,128)}, f32[8,128,64]{2,1,0:T(8,128)S(1)}, f32[8,128,64]{2,1,0:T(8,128)}, f32[8,128,64]{2,1,0:T(8,128)S(1)}) fusion(f32[8,128,384]{2,1,0:T(8,128)S(1)} %fusion.76), kind=kLoop, calls=%fused_computation.69.clone.1 | loop fusion | bytes 2097152 | tf_op jit(solution)/shard_map/while/body/eval_jaxpr/while/body/eval_jaxpr/slice | solution.py:45
  79.1 1.9 %copy.84 = f32[8,128,64]{1,2,0:T(8,128)} copy(f32[8,128,64]{2,1,0:T(8,128)} %get-tuple-element.272) | data formatting | bytes 524288 | tf_op jit(solution)/shard_map/while/body/eval_jaxpr/while
  81.0 1.9 %copy.85 = f32[8,128,64]{1,2,0:T(8,128)} copy(f32[8,128,64]{2,1,0:T(8,128)} %get-tuple-element.273) | data formatting | bytes 524288 | tf_op jit(solution)/shard_map/while/body/eval_jaxpr/while
  83.0 0.9 copy.86
  84.0 0.5 compare_convert_fusion.4
  84.6 0.5 compare_convert_fusion.5
  85.2 1.3 multiply_convert_fusion.5
  86.5 0.7 copy.88
  87.2 3.5 %all-to-all-start = ((bf16[8,128,64]{1,0,2:T(8,128)(2,1)}), bf16[8,128,64]{1,0,2:T(8,128)(2,1)S(1)}, u32[]{:S(2)}, u32[]{:S(2)}) async-start(bf16[8,128,64]{1,0,2:T(8,128)(2,1)} %copy.88), calls=%async_computation | async-start | bytes 262144 | tf_op jit(solution)/shard_map/while/body/eval_jaxpr/while/body/eval_jaxpr/all_to_all | solution.py:49
  90.8 7.8 %all-to-all-done = bf16[8,128,64]{1,0,2:T(8,128)(2,1)S(1)} async-done(((bf16[8,128,64]{1,0,2:T(8,128)(2,1)}), bf16[8,128,64]{1,0,2:T(8,128)(2,1)S(1)}, u32[]{:S(2)}, u32[]{:S(2)}) %all-to-all-start) | async-done | bytes 131104 | tf_op jit(solution)/shard_map/while/body/eval_jaxpr/while/body/eval_jaxpr/all_to_all | solution.py:49
  98.6 10.5 %all_to_all.88 = bf16[8,128,64]{1,0,2:T(8,128)(2,1)S(1)} all-to-all(bf16[8,128,64]{1,0,2:T(8,128)(2,1)S(1)} %copy.89), channel_id=1, replica_groups=mesh['section'=2,'row'=16] {'row'}, dimensions={2} | all-to-all | bytes 262144 | tf_op jit(solution)/shard_map/while/body/eval_jaxpr/while/body/eval_jaxpr/all_to_all | solution.py:50
  109.3 0.8 copy.90
  110.1 3.5 %all-to-all-start.2 = ((bf16[128,128,4]{1,2,0:T(4,128)(2,1)}), bf16[128,128,4]{1,2,0:T(4,128)(2,1)S(1)}, u32[]{:S(2)}, u32[]{:S(2)}) async-start(bf16[128,128,4]{1,2,0:T(4,128)(2,1)} %copy.90), calls=%async_computation.2 | async-start | bytes 262144 | tf_op jit(solution)/shard_map/while/body/eval_jaxpr/while/body/eval_jaxpr/all_to_all | solution.py:55
  113.6 7.9 %all-to-all-done.2 = bf16[128,128,4]{1,2,0:T(4,128)(2,1)S(1)} async-done(((bf16[128,128,4]{1,2,0:T(4,128)(2,1)}), bf16[128,128,4]{1,2,0:T(4,128)(2,1)S(1)}, u32[]{:S(2)}, u32[]{:S(2)}) %all-to-all-start.2) | async-done | bytes 131104 | tf_op jit(solution)/shard_map/while/body/eval_jaxpr/while/body/eval_jaxpr/all_to_all | solution.py:55
  121.7 0.4 fusion.82
  122.9 0.7 fusion.83
  123.7 0.7 fusion.84
  124.6 0.4 fusion.85
  125.1 0.7 copy-done.1
  (56 shorter events, 4.4 us)
Async XLA Ops:
  0.0 23.4 %copy-start = (bf16[2,8,128,128]{3,2,1,0:T(8,128)(2,1)S(1)}, bf16[2,8,128,128]{3,2,1,0:T(8,128)(2,1)}, u32[]{:S(2)}) copy-start(bf16[2,8,128,128]{3,2,1,0:T(8,128)(2,1)} %param.9) | copy-start | bytes 1572868
  0.0 23.5 %collective-permute-start = (bf16[1,128,1024]{2,1,0:T(8,128)(2,1)}, bf16[1,128,1024]{2,1,0:T(8,128)(2,1)S(1)}, u32[]{:S(2)}, u32[]{:S(2)}) collective-permute-start(bf16[1,128,1024]{2,1,0:T(8,128)(2,1)} %param.14), channel_id=1, source_target_pairs={{0,16},{16,0},{1,17},{17,1},{2,18},{18,2},{3,19},{19,3},{4,20},{20... | collective-permute-start | bytes 786440 | tf_op jit(solution)/shard_map/ppermute | solution.py:15
  25.6 0.7 copy-start.4
  36.3 13.8 %all-to-all-start = ((bf16[8,128,64]{1,0,2:T(8,128)(2,1)}), bf16[8,128,64]{1,0,2:T(8,128)(2,1)S(1)}, u32[]{:S(2)}, u32[]{:S(2)}) async-start(bf16[8,128,64]{1,0,2:T(8,128)(2,1)} %copy.88), calls=%async_computation | async-start | bytes 262144 | tf_op jit(solution)/shard_map/while/body/eval_jaxpr/while/body/eval_jaxpr/all_to_all | solution.py:49
  61.6 11.4 %all-to-all-start.2 = ((bf16[128,128,4]{1,2,0:T(4,128)(2,1)}), bf16[128,128,4]{1,2,0:T(4,128)(2,1)S(1)}, u32[]{:S(2)}, u32[]{:S(2)}) async-start(bf16[128,128,4]{1,2,0:T(4,128)(2,1)} %copy.90), calls=%async_computation.2 | async-start | bytes 262144 | tf_op jit(solution)/shard_map/while/body/eval_jaxpr/while/body/eval_jaxpr/all_to_all | solution.py:55
  73.2 1.2 copy-start.2
  75.1 1.0 copy-start.3
  75.1 1.4 %copy-start.5 = (bf16[2,128,384]{2,1,0:T(8,128)(2,1)S(1)}, bf16[2,128,384]{2,1,0:T(8,128)(2,1)}, u32[]{:S(2)}) copy-start(bf16[2,128,384]{2,1,0:T(8,128)(2,1)} %copy-done.4) | copy-start | bytes 589828 | tf_op jit(solution)/shard_map/while/body/eval_jaxpr/while
  76.5 0.7 copy-start.4
  87.2 11.4 %all-to-all-start = ((bf16[8,128,64]{1,0,2:T(8,128)(2,1)}), bf16[8,128,64]{1,0,2:T(8,128)(2,1)S(1)}, u32[]{:S(2)}, u32[]{:S(2)}) async-start(bf16[8,128,64]{1,0,2:T(8,128)(2,1)} %copy.88), calls=%async_computation | async-start | bytes 262144 | tf_op jit(solution)/shard_map/while/body/eval_jaxpr/while/body/eval_jaxpr/all_to_all | solution.py:49
  110.1 11.4 %all-to-all-start.2 = ((bf16[128,128,4]{1,2,0:T(4,128)(2,1)}), bf16[128,128,4]{1,2,0:T(4,128)(2,1)S(1)}, u32[]{:S(2)}, u32[]{:S(2)}) async-start(bf16[128,128,4]{1,2,0:T(4,128)(2,1)} %copy.90), calls=%async_computation.2 | async-start | bytes 262144 | tf_op jit(solution)/shard_map/while/body/eval_jaxpr/while/body/eval_jaxpr/all_to_all | solution.py:55
  121.7 1.2 copy-start.2
  123.6 1.0 copy-start.3
  123.7 1.4 %copy-start.5 = (bf16[2,128,384]{2,1,0:T(8,128)(2,1)S(1)}, bf16[2,128,384]{2,1,0:T(8,128)(2,1)}, u32[]{:S(2)}) copy-start(bf16[2,128,384]{2,1,0:T(8,128)(2,1)} %copy-done.4) | copy-start | bytes 589828 | tf_op jit(solution)/shard_map/while/body/eval_jaxpr/while
  125.1 0.7 copy-start.1
